TPU v7x, 32 devices: a whole 2x2x4 slice. The times are simulated.
32 devices in a mesh: ha: 8 (over z, core), gz: 4 (over y, x).
Axes of the slice: x: 2, y: 2, z: 4, core: 2. Of those that a mesh axis runs over, the one named last changes fastest.
Arguments:
- velocity: bfloat16 [16, 2048, 2048], P('gz', 'ha'), may hold values from -48 to 48
- lower_coef: float32 [16], P('gz'), may hold values from 200 to 20000
- upper_coef: float32 [16], P('gz'), may hold values from 200 to 20000
Outputs:
- diffused: bfloat16 [16, 2048, 2048], P('gz', 'ha')
All inputs are finite; a program needn't handle non-finite values.
Results may differ from a plain program's by a relative error of at most 0.012.
The roundings to bfloat16 on the way count: a program that leaves them out, or rounds other values in their place, can miss the bound.
Values may be sent and summed in bfloat16 or wider, within the bound.
A program may use at most 64 MiB of HBM per device.

v0:
```python
import math

import jax
import jax.numpy as jnp
from jax import lax
from jax.sharding import PartitionSpec as P

NX = 2048
NY = 2048
KYW = 128


wavenumber_scale = 0.001


def tables(length, mode_count):
    position = jnp.arange(length, dtype=jnp.int32)[:, None]
    wave_index = jnp.arange(mode_count, dtype=jnp.int32)[None, :]
    angles = (position * wave_index % length).astype(jnp.float32) * (2.0 * math.pi / length)
    factor = 1.0 / math.sqrt(length)
    return (
        (jnp.cos(angles) * factor).astype(jnp.bfloat16),
        (jnp.sin(angles) * factor).astype(jnp.bfloat16),
    )


def signed_wave(lane_index):
    return jnp.where(lane_index < NX // 2, lane_index, lane_index - NX).astype(jnp.float32)


def damping_for(kx_value, spanwise_wave_value):
    return 1.0 + wavenumber_scale * (
        kx_value[None, :] * kx_value[None, :]
        + spanwise_wave_value[:, None] * spanwise_wave_value[:, None]
    )


def band_pair(lower_coef, upper_coef, z_global, z_total):
    sub_coef = jnp.where(z_global == 0, jnp.zeros_like(lower_coef), -lower_coef)
    sup_coef = jnp.where(z_global == z_total - 1, jnp.zeros_like(upper_coef), -upper_coef)
    return (sub_coef, sup_coef)


def thomas(lower_band, main_band, upper_band, source):

    def forward(running, packed):
        upper_prev, previous_source = running
        lower_row, main_row, upper_row, source_row = packed
        inverse = 1.0 / (main_row - lower_row * upper_prev)
        upper_new = upper_row * inverse
        source_new = (source_row - lower_row[None] * previous_source) * inverse[None]
        return ((upper_new, source_new), (upper_new, source_new))

    initial = (jnp.zeros_like(main_band[0]), jnp.zeros_like(source[0]))
    unused, (upper_mod, source_mod) = lax.scan(
        forward, initial, (lower_band, main_band, upper_band, source)
    )

    def backward(running, packed):
        upper_row, source_row = packed
        result = source_row - upper_row[None] * running
        return (result, result)

    unused, solved = lax.scan(
        backward, jnp.zeros_like(source[0]), (upper_mod, source_mod), reverse=True
    )
    return solved


def body(velocity, lower_coef, upper_coef):
    depth_rows = velocity.shape[0]
    z_groups = lax.axis_size("gz")
    z_total = depth_rows * z_groups
    wave_count = KYW // lax.axis_size("ha")
    y_cosine, y_sine = tables(NY, KYW)
    x_cosine, x_sine = tables(NX, NX)
    spec_re = jnp.einsum("zxy,yk->zkx", velocity, y_cosine, preferred_element_type=jnp.float32)
    spec_im = -jnp.einsum("zxy,yk->zkx", velocity, y_sine, preferred_element_type=jnp.float32)
    spectrum = jnp.stack([spec_re, spec_im], 1).astype(jnp.bfloat16)
    block = lax.all_to_all(spectrum, "ha", split_axis=2, concat_axis=3, tiled=True)
    with_cos = jnp.dot(block, x_cosine, preferred_element_type=jnp.float32)
    with_sin = jnp.dot(block, x_sine, preferred_element_type=jnp.float32)
    source = jnp.stack([with_cos[:, 0] + with_sin[:, 1], with_cos[:, 1] - with_sin[:, 0]], 1)
    spanwise_wave_value = (
        lax.axis_index("ha") * wave_count + jnp.arange(wave_count, dtype=jnp.int32)
    ).astype(jnp.float32)
    lower_all, upper_all = (
        lax.all_gather(lower_coef, "gz", axis=0, tiled=True),
        lax.all_gather(upper_coef, "gz", axis=0, tiled=True),
    )
    columns = lax.all_to_all(source, "gz", split_axis=3, concat_axis=0, tiled=True)
    lane_count = NX // z_groups
    lane_index = lax.axis_index("gz") * lane_count + jnp.arange(lane_count, dtype=jnp.int32)
    z_every = jnp.arange(z_total, dtype=jnp.int32)
    sub_coef, sup_coef = band_pair(lower_all, upper_all, z_every, z_total)
    main_band = (
        damping_for(signed_wave(lane_index), spanwise_wave_value)[None]
        + (lower_all + upper_all)[:, None, None]
    )
    sub_band = jnp.broadcast_to(sub_coef[:, None, None], main_band.shape)
    sup_band = jnp.broadcast_to(sup_coef[:, None, None], main_band.shape)
    solved_columns = thomas(sub_band, main_band, sup_band, columns)
    solved = lax.all_to_all(
        solved_columns.astype(jnp.bfloat16), "gz", split_axis=0, concat_axis=3, tiled=True
    ).astype(solved_columns.dtype)
    rounded = solved.astype(jnp.bfloat16)
    part_cos = jnp.dot(rounded, x_cosine, preferred_element_type=jnp.float32)
    part_sin = jnp.dot(rounded, x_sine, preferred_element_type=jnp.float32)
    planes = jnp.stack(
        [part_cos[:, 0] - part_sin[:, 1], part_cos[:, 1] + part_sin[:, 0]], 1
    ).astype(jnp.bfloat16)
    weight = jnp.where(jnp.arange(KYW, dtype=jnp.int32) == 0, 1.0, 2.0).astype(jnp.float32)
    w_cosine = (y_cosine.astype(jnp.float32) * weight[None, :]).astype(jnp.bfloat16)
    w_sine = (y_sine.astype(jnp.float32) * weight[None, :]).astype(jnp.bfloat16)
    block = lax.all_to_all(planes, "ha", split_axis=3, concat_axis=2, tiled=True)
    result = jnp.einsum("nkx,yk->nxy", block[:, 0], w_cosine, preferred_element_type=jnp.float32)
    result = result - jnp.einsum(
        "nkx,yk->nxy", block[:, 1], w_sine, preferred_element_type=jnp.float32
    )
    return result.astype(jnp.bfloat16)


def solution(mesh):
    in_specs = (P("gz", "ha", None), P("gz"), P("gz"))
    out_specs = P("gz", "ha", None)
    return jax.shard_map(body, mesh=mesh, in_specs=in_specs, out_specs=out_specs, check_vma=False)
```

profile of v0, /device:TPU:0, one launch (start us, length us, event | category | flops | bytes accessed | tf_op | source)
XLA Modules:
  0.0 463.0 jit_solution(8964159835763546715)
XLA Ops:
  0.0 6.9 %fusion.19 = bf16[4,1,128,256]{3,2,0,1:T(8,128)(2,1)S(1)} fusion(bf16[4,256,2048]{2,1,0:T(8,128)(2,1)} %param.7), kind=kOutput, calls=%fused_computation.38 | convolution fusion | flops 541196288 | bytes 4456448 | tf_op jit(solution)/shard_map/zxy,yk->zkx/dot_general | solution.py:77
  6.9 4.9 %fusion.20 = bf16[4,1,128,256]{3,2,0,1:T(8,128)(2,1)S(1)} fusion(bf16[4,256,2048]{2,1,0:T(8,128)(2,1)S(1)} %copy-done), kind=kOutput, calls=%fused_computation.39 | convolution fusion | flops 541327360 | bytes 4456448 | tf_op jit(solution)/shard_map/zxy,yk->zkx/dot_general | solution.py:78
  13.0 6.4 %all-to-all-start = ((bf16[4,2,128,256]{3,0,1,2:T(4,128)(2,1)}), bf16[4,2,128,256]{3,0,1,2:T(4,128)(2,1)S(1)}, u32[]{:S(2)}, u32[]{:S(2)}) async-start(bf16[4,2,128,256]{3,0,1,2:T(4,128)(2,1)} %copy.30), calls=%async_computation | async-start | bytes 1048576 | tf_op jit(solution)/shard_map/all_to_all | solution.py:80
  21.0 10.2 %all-reduce.2 = (f32[16]{0:T(128)S(1)}, f32[16]{0:T(128)S(1)}) all-reduce(f32[16]{0:T(128)S(1)} %dynamic-update-slice, f32[16]{0:T(128)S(1)} %dynamic-update-slice.1), channel_id=1, replica_groups=mesh['ha'=8,'gz'=4] {'gz'}, use_global_device_ids=true, to_apply=%add | all-reduce | flops 32 | bytes 256
  31.3 3.4 all-to-all-done
  35.3 63.3 %fusion.12 = f32[4,2,16,2048]{3,2,1,0:T(8,128)S(1)} fusion(bf16[4,2,16,2048]{3,2,1,0:T(8,128)(2,1)S(1)} %all_to_all.55), kind=kOutput, calls=%fused_computation.29 | convolution fusion | flops 1140850688 | bytes 1572864 | tf_op jit(solution)/shard_map/dot_general | solution.py:82
  98.6 63.3 %fusion.16 = f32[4,2,16,2048]{3,2,1,0:T(8,128)S(1)} fusion(bf16[4,2,16,2048]{3,2,1,0:T(8,128)(2,1)S(1)} %all_to_all.55), kind=kOutput, calls=%fused_computation.31 | convolution fusion | flops 1140850688 | bytes 1572864 | tf_op jit(solution)/shard_map/dot_general | solution.py:81
  162.1 8.5 %copy.32 = f32[4,2,16,2048]{2,1,0,3:T(2,128)} copy(f32[4,2,16,2048]{3,2,1,0:T(8,128)S(1)} %pad_maximum_fusion) | data formatting | bytes 2097152 | tf_op jit(solution)/shard_map/stack | solution.py:83
  170.6 13.5 %reshape.71 = f32[4,1,65536]{2,1,0:T(1,128)} reshape(f32[2048,4,2,16]{3,2,1,0:T(2,128)} %bitcast.113) | data formatting | bytes 2097152
  184.1 3.9 all-to-all-start.1
  188.2 13.1 %all-to-all-done.1 = f32[4,1,65536]{2,1,0:T(1,128)S(1)} async-done(((f32[4,1,65536]{2,1,0:T(1,128)}), f32[4,1,65536]{2,1,0:T(1,128)S(1)}, u32[]{:S(2)}, u32[]{:S(2)}) %all-to-all-start.1) | async-done | bytes 1048608 | tf_op jit(solution)/shard_map/all_to_all | solution.py:91
  201.9 3.7 reduce
  205.6 14.1 %reshape.72 = f32[2048,4,2,16]{3,2,1,0:T(2,128)} reshape(f32[4,65536]{1,0:T(4,128)S(1)} %reduce) | data formatting | bytes 2097152
  219.7 10.1 %copy.33 = f32[4,4,2,16,512]{4,3,2,1,0:T(8,128)S(1)} copy(f32[4,4,2,16,512]{3,2,1,4,0:T(2,128)} %bitcast.114) | data formatting | bytes 2097152 | tf_op jit(solution)/shard_map/all_to_all | solution.py:91
  231.8 23.1 %while.34 = (s32[]{:T(128)}, f32[16,512]{1,0:T(8,128)S(1)}, f32[2,16,512]{2,1,0:T(8,128)S(1)}, f32[16,16,512]{2,1,0:T(8,128)}, f32[16,2,16,512]{3,2,1,0:T(8,128)...) while((s32[]{:T(128)}, f32[16,512]{1,0:T(8,128)S(1)}, ...), condition=%wide.region_1.2_spmd.clone, body=%wide.region_0.1_spmd.clone.sunk | while | flops 106499 | bytes 590460 | solution.py:55
  231.8 1.4 bitcast_dynamic-update-slice_fusion.6
  236.1 1.4 bitcast_dynamic-update-slice_fusion.6
  237.6 1.4 bitcast_dynamic-update-slice_fusion.6
  249.1 1.4 bitcast_dynamic-update-slice_fusion.6
  252.0 1.4 bitcast_dynamic-update-slice_fusion.6
  254.9 13.0 %while.35 = (s32[]{:T(128)}, f32[2,16,512]{2,1,0:T(8,128)S(1)}, bf16[16,2,16,512]{3,2,1,0:T(8,128)(2,1)S(1)}, f32[16,2,16,512]{3,2,1,0:T(8,128)S(1)}, f32[16,16,...) while((s32[]{:T(128)}, f32[2,16,512]{2,1,0:T(8,128)S(1)}, ...), condition=%wide.region_3.4_spmd.clone, body=%wide.region_2.3_spmd.clone.sunk | while | flops 49156 | bytes 360563 | solution.py:64
  267.9 10.7 %all_to_all.72 = bf16[16,2,16,512]{3,2,1,0:T(8,128)(2,1)S(1)} all-to-all(bf16[16,2,16,512]{3,2,1,0:T(8,128)(2,1)S(1)} %get-tuple-element.158), channel_id=1, replica_groups=mesh['ha'=8,'gz'=4] {'gz'}, dimensions={0} | all-to-all | bytes 1048576 | tf_op jit(solution)/shard_map/all_to_all | solution.py:103
  279.3 63.3 %fusion.10 = f32[4,2,16,2048]{3,2,1,0:T(8,128)S(1)} fusion(bf16[4,2,16,2048]{3,2,1,0:T(8,128)(2,1)S(1)} %all_to_all.63), kind=kOutput, calls=%fused_computation.28 | convolution fusion | flops 1140850688 | bytes 1572864 | tf_op jit(solution)/shard_map/dot_general | solution.py:108
  342.7 63.2 %fusion.14 = f32[4,2,16,2048]{3,2,1,0:T(8,128)S(1)} fusion(bf16[4,2,16,2048]{3,2,1,0:T(8,128)(2,1)S(1)} %all_to_all.63), kind=kOutput, calls=%fused_computation.30 | convolution fusion | flops 1140850688 | bytes 1572864 | tf_op jit(solution)/shard_map/dot_general | solution.py:107
  406.0 7.3 %copy.35 = bf16[4,2,16,2048]{2,1,0,3:T(2,128)(2,1)} copy(bf16[4,2,16,2048]{3,2,1,0:T(8,128)(2,1)S(1)} %pad_maximum_fusion.2) | data formatting | bytes 1048576 | tf_op jit(solution)/shard_map/stack | solution.py:109
  413.3 6.4 %reshape.73 = bf16[8,2,16384]{2,1,0:T(2,128)(2,1)} reshape(bf16[2048,4,2,16]{3,2,1,0:T(2,128)(2,1)} %bitcast.115) | data formatting | bytes 1048576
  419.8 3.7 all-to-all-start.3
  423.4 15.2 %all-to-all-done.3 = bf16[8,2,16384]{2,1,0:T(2,128)(2,1)S(1)} async-done(((bf16[8,2,16384]{2,1,0:T(2,128)(2,1)}), bf16[8,2,16384]{2,1,0:T(2,128)(2,1)S(1)}, u32[]{:S(2)}, u32[]{:S(2)}) %all-to-all-start.3) | async-done | bytes 524320 | tf_op jit(solution)/shard_map/all_to_all | solution.py:115
  438.7 4.1 reshape.74
  442.7 8.9 %copy.47 = bf16[4,2,16,8,256]{4,2,3,1,0:T(8,128)(2,1)S(1)} copy(bf16[4,2,16,8,256]{2,1,0,4,3:T(2,128)(2,1)} %bitcast.116) | data formatting | bytes 1048576 | tf_op jit(solution)/shard_map/all_to_all | solution.py:115
  451.6 4.7 %fusion.28 = f32[4,256,2048]{2,1,0:T(8,128)S(1)} fusion(f32[128]{0:T(128)S(1)} %compare_select_fusion.1, bf16[4,2,128,256]{3,2,1,0:T(8,128)(2,1)S(1)} %bitcast.117), kind=kOutput, calls=%fused_computation.52 | convolution fusion | flops 541851648 | bytes 8651264 | tf_op jit(solution)/shard_map/nkx,yk->nxy/dot_general | solution.py:116
  456.3 6.5 %subtract_convert_fusion = bf16[4,256,2048]{2,1,0:T(8,128)(2,1)} fusion(f32[4,256,2048]{2,1,0:T(8,128)S(1)} %fusion.28, f32[128]{0:T(128)S(1)} %compare_select_fusion.1, bf16[4,2,128,256]{3,2,1,0:T(8,128)(2,1)S(1)} %bitcast.118), kind=kOutput, calls=%fused_computation.27 | convolution fusion | flops 546045952 | bytes 12845568 | tf_op jit(solution)/shard_map/nkx,yk->nxy/dot_general | solution.py:117
  (97 shorter events, 35.3 us)
Async XLA Ops:
  0.0 19.4 %copy-start.3 = (u32[32]{0:T(128)S(1)}, u32[32]{0:T(128)}, u32[]{:S(2)}) copy-start(u32[32]{0:T(128)} %constant.120) | copy-start | bytes 388
  0.0 6.9 %copy-start = (bf16[4,256,2048]{2,1,0:T(8,128)(2,1)S(1)}, bf16[4,256,2048]{2,1,0:T(8,128)(2,1)}, u32[]{:S(2)}) copy-start(bf16[4,256,2048]{2,1,0:T(8,128)(2,1)} %param.7) | copy-start | bytes 12582916
  0.0 20.5 %copy-start.1 = (f32[4]{0:T(128)S(1)}, f32[4]{0:T(128)}, u32[]{:S(2)}) copy-start(f32[4]{0:T(128)} %param.9) | copy-start | bytes 52
  0.0 20.8 %copy-start.2 = (f32[4]{0:T(128)S(1)}, f32[4]{0:T(128)}, u32[]{:S(2)}) copy-start(f32[4]{0:T(128)} %param.8) | copy-start | bytes 52
  13.0 21.7 %all-to-all-start = ((bf16[4,2,128,256]{3,0,1,2:T(4,128)(2,1)}), bf16[4,2,128,256]{3,0,1,2:T(4,128)(2,1)S(1)}, u32[]{:S(2)}, u32[]{:S(2)}) async-start(bf16[4,2,128,256]{3,0,1,2:T(4,128)(2,1)} %copy.30), calls=%async_computation | async-start | bytes 1048576 | tf_op jit(solution)/shard_map/all_to_all | solution.py:80
  184.1 17.3 %all-to-all-start.1 = ((f32[4,1,65536]{2,1,0:T(1,128)}), f32[4,1,65536]{2,1,0:T(1,128)S(1)}, u32[]{:S(2)}, u32[]{:S(2)}) async-start(f32[4,1,65536]{2,1,0:T(1,128)} %reshape.71), calls=%async_computation.1 | async-start | bytes 2097152 | tf_op jit(solution)/shard_map/all_to_all | solution.py:91
  419.8 18.9 %all-to-all-start.3 = ((bf16[8,2,16384]{2,1,0:T(2,128)(2,1)}), bf16[8,2,16384]{2,1,0:T(2,128)(2,1)S(1)}, u32[]{:S(2)}, u32[]{:S(2)}) async-start(bf16[8,2,16384]{2,1,0:T(2,128)(2,1)} %reshape.73), calls=%async_computation.3 | async-start | bytes 1048576 | tf_op jit(solution)/shard_map/all_to_all | solution.py:115
where the time goes:
time: 471 us; the launch traced here: 463 us
  matrix products  276 us (59%)
  local copies, waits for them, and re-layouts  91.2 us (19%)
  waiting for transfers between devices  31.8 us (7%)
  other arithmetic  27.7 us (6%)
  blocking collectives  20.8 us (4%)
  starting transfers between devices  13.9 us (3%)
    dot_general x1, matrix products, body(): with_sin = jnp.dot(block, x_sine, preferred_element_type=jnp.float32)  63.3 us
    dot_general x1, matrix products, body(): part_sin = jnp.dot(rounded, x_sine, preferred_element_type=jnp.float32)  63.3 us
    dot_general x1, matrix products, body(): with_cos = jnp.dot(block, x_cosine, preferred_element_type=jnp.float32)  63.3 us
    dot_general x1, matrix products, body(): part_cos = jnp.dot(rounded, x_cosine, preferred_element_type=jnp.float32)  63.2 us
    unnamed x15, local copies, waits for them, and re-layouts  39.2 us
    dynamic_update_slice x48, other arithmetic, thomas(): lax.scan(forward, initial, (lower_band, main_band, upper_band, source))  23.4 us
    all_to_all x1, waiting for transfers between devices, body(): lax.all_to_all(planes, 'ha', split_axis=3, concat_axis=2, tiled=True)  15.2 us
    all_to_all x1, waiting for transfers between devices, body(): lax.all_to_all(source, 'gz', split_axis=3, concat_axis=0, tiled=True)  13.1 us
  transfers between devices with their start and end apart: 3, of which 3 were waited for; matrix products, arithmetic and copies ran while one was open for 0% of the time, Pallas kernels for 0%

commit v1 on v0

--- a/solution.py
+++ b/solution.py
@@ -1,13 +1,19 @@
+import functools
 import math
 
 import jax
 import jax.numpy as jnp
+import numpy as np
 from jax import lax
+from jax.experimental import pallas as pl
+from jax.experimental.pallas import tpu as pltpu
 from jax.sharding import PartitionSpec as P
 
 NX = 2048
 NY = 2048
 KYW = 128
+GROUP = 8
+LANES = 128
 
 
 wavenumber_scale = 0.001
@@ -67,7 +73,7 @@
     return solved
 
 
-def body(velocity, lower_coef, upper_coef):
+def body_general(velocity, lower_coef, upper_coef):
     depth_rows = velocity.shape[0]
     z_groups = lax.axis_size("gz")
     z_total = depth_rows * z_groups
@@ -120,7 +126,327 @@
     return result.astype(jnp.bfloat16)
 
 
+def host_tables(length, mode_count):
+    position = np.arange(length)[:, None]
+    wave_index = np.arange(mode_count)[None, :]
+    angles = (position * wave_index % length) * (2.0 * math.pi / length)
+    factor = 1.0 / math.sqrt(length)
+    return np.cos(angles) * factor, np.sin(angles) * factor
+
+
+def real_x_table():
+    cosine, sine = host_tables(NX, NX // 2 + 1)
+    half = NX // 2
+    table = np.concatenate([cosine[:, :half], sine[:, :half]], 1)
+    table[:, half] = cosine[:, half]
+    return jnp.asarray(table, jnp.bfloat16)
+
+
+def other_half_first(position, step, count):
+    half = count // 2
+    side = position // half
+    base = jnp.where(step < half, (1 - side) * half, side * half)
+    return base + (position + 1 + step) % half
+
+
+def own_half_first(position, step, count):
+    half = count // 2
+    side = position // half
+    base = jnp.where(step < half, side * half, (1 - side) * half)
+    return base + (position + step) % half
+
+
+def middle_kernel(
+    n_ha, n_gz, depth,
+    velocity_ref, y_table_ref, x_table_ref, lower_ref, upper_ref,
+    out_ref,
+    velocity, y_table, x_table, send1, recv1, wave, inverse, upper_mod, solved,
+    send2, recv2, coef, coefs,
+    load_sem, table_sem, own_sem,
+    send1_sem, recv1_sem, send2_sem, recv2_sem, coef_send_sem, coef_recv_sem,
+):
+    ha = lax.axis_index("ha")
+    gz = lax.axis_index("gz")
+    count = n_ha * n_gz
+    me = ha * n_gz + gz
+    rows = velocity.shape[1]
+    z_total = depth * n_gz
+    block_rows = depth * GROUP
+    bulk = z_total * GROUP
+    half_ha = n_ha // 2
+    half_channels = half_ha * n_gz * GROUP
+
+    y_load = pltpu.make_async_copy(y_table_ref, y_table, load_sem.at[depth])
+    y_load.start()
+    loads = []
+    for z in range(depth):
+        load = pltpu.make_async_copy(velocity_ref.at[z], velocity.at[z], load_sem.at[z])
+        load.start()
+        loads.append(load)
+    x_load = pltpu.make_async_copy(x_table_ref, x_table, table_sem)
+    x_load.start()
+
+    barrier = pltpu.get_barrier_semaphore()
+
+    @pl.loop(1, count)
+    def _(step):
+        peer = (me + step) % count
+        pl.semaphore_signal(
+            barrier, inc=1, device_id={"ha": peer // n_gz, "gz": peer % n_gz},
+            device_id_type=pl.DeviceIdType.MESH,
+        )
+
+    for z in range(depth):
+        coef[pl.ds(z, 1), :] = jnp.full((1, LANES), lower_ref[z], jnp.float32)
+        coef[pl.ds(depth + z, 1), :] = jnp.full((1, LANES), upper_ref[z], jnp.float32)
+
+    def first_copy(h, g, slot_h, slot_g):
+        return pltpu.make_async_remote_copy(
+            src_ref=send1.at[h, g],
+            dst_ref=recv1.at[slot_h, slot_g],
+            send_sem=send1_sem.at[h * n_gz + g],
+            recv_sem=recv1_sem.at[slot_h * n_gz + slot_g],
+            device_id={"ha": h, "gz": g},
+            device_id_type=pl.DeviceIdType.MESH,
+        )
+
+    def second_copy(h, g, slot):
+        return pltpu.make_async_remote_copy(
+            src_ref=send2.at[h, g],
+            dst_ref=recv2.at[slot],
+            send_sem=send2_sem.at[h * n_gz + g],
+            recv_sem=recv2_sem.at[slot],
+            device_id={"ha": h, "gz": g},
+            device_id_type=pl.DeviceIdType.MESH,
+        )
+
+    def coef_copy(g, slot):
+        return pltpu.make_async_remote_copy(
+            src_ref=coef,
+            dst_ref=coefs.at[slot],
+            send_sem=coef_send_sem.at[g],
+            recv_sem=coef_recv_sem.at[slot],
+            device_id={"ha": ha, "gz": g},
+            device_id_type=pl.DeviceIdType.MESH,
+        )
+
+    y_load.wait()
+    for part in range(2):
+        side = (ha // half_ha + 1 + part) % 2
+        first = pl.multiple_of(side * half_channels, half_channels)
+        planes = []
+        for z in range(depth):
+            if part == 0:
+                loads[z].wait()
+            planes.append(
+                lax.dot_general(
+                    y_table[pl.ds(first, half_channels), :], velocity[z],
+                    (((1,), (1,)), ((), ())), preferred_element_type=jnp.float32,
+                ).reshape(half_ha, n_gz, 1, GROUP, rows)
+            )
+        spectrum = jnp.concatenate(planes, 2).reshape(half_ha, n_gz, block_rows, rows)
+        send1[pl.ds(side * half_ha, half_ha)] = spectrum.astype(jnp.bfloat16)
+
+        if part == 0:
+            pl.semaphore_wait(barrier, count - 1)
+
+            @pl.loop(1, n_gz)
+            def _(step):
+                coef_copy((gz + step) % n_gz, gz).start()
+
+        @pl.loop(0, half_ha * n_gz)
+        def _(step):
+            h = side * half_ha + (ha + 1 + step // n_gz) % half_ha
+            g = (gz + 1 + step) % n_gz
+
+            @pl.when(h * n_gz + g != me)
+            def _():
+                first_copy(h, g, ha, gz).start()
+
+    own = pltpu.make_async_copy(send1.at[ha, gz], recv1.at[ha, gz], own_sem.at[0])
+    own.start()
+    own_coef = pltpu.make_async_copy(coef, coefs.at[gz], own_sem.at[1])
+    own_coef.start()
+
+    own_coef.wait()
+
+    @pl.loop(1, n_gz)
+    def _(step):
+        g = (gz + step) % n_gz
+        coef_copy(g, g).wait_recv()
+
+    width = 4 * LANES
+    channel = me * GROUP + lax.broadcasted_iota(jnp.int32, (GROUP, width), 0)
+    spanwise = (channel % KYW).astype(jnp.float32)
+
+    def spread(row):
+        return jnp.tile(row, (GROUP, width // LANES))
+
+    lower_of = lambda z: coefs[z // depth, pl.ds(z % depth, 1), :]
+    upper_of = lambda z: coefs[z // depth, pl.ds(depth + z % depth, 1), :]
+
+    @pl.loop(0, NX // width)
+    def _(piece):
+        at = pl.ds(pl.multiple_of(piece * width, width), width)
+        column = piece * width + lax.broadcasted_iota(jnp.int32, (GROUP, width), 1)
+        half = NX // 2
+        wave_number = jnp.where(column <= half, column, column - half).astype(jnp.float32)
+        damping = 1.0 + wavenumber_scale * (wave_number * wave_number + spanwise * spanwise)
+        previous = None
+        for z in range(z_total):
+            lower, upper = spread(lower_of(z)), spread(upper_of(z))
+            pivot = damping + (lower + upper)
+            if z > 0:
+                pivot = pivot + lower * previous
+            inv = 1.0 / pivot
+            inverse[pl.ds(z * GROUP, GROUP), at] = inv
+            previous = -upper * inv
+            upper_mod[pl.ds(z * GROUP, GROUP), at] = previous
+
+    own.wait()
+    x_load.wait()
+    wave[...] = jnp.zeros_like(wave)
+
+    @pl.loop(0, n_ha)
+    def _(step):
+        h = own_half_first(ha, step, n_ha)
+
+        @pl.loop(0, n_gz)
+        def _(g):
+            @pl.when(h * n_gz + g != me)
+            def _():
+                first_copy(h, g, h, g).wait_recv()
+
+        wave[...] += jnp.dot(
+            recv1[h].reshape(bulk, rows),
+            x_table[pl.ds(pl.multiple_of(h * rows, rows), rows), :],
+            preferred_element_type=jnp.float32,
+        )
+
+    @pl.loop(0, NX // width)
+    def _(piece):
+        at = pl.ds(pl.multiple_of(piece * width, width), width)
+        column = piece * width + lax.broadcasted_iota(jnp.int32, (GROUP, width), 1)
+        weight = jnp.where(column % (NX // 2) == 0, 1.0, 2.0).astype(jnp.float32)
+        value = None
+        forward = []
+        for z in range(z_total):
+            source = wave[pl.ds(z * GROUP, GROUP), at]
+            if z > 0:
+                source = source + spread(lower_of(z)) * value
+            value = source * inverse[pl.ds(z * GROUP, GROUP), at]
+            wave[pl.ds(z * GROUP, GROUP), at] = value
+        later = value * weight
+        for z in range(z_total - 2, -1, -2):
+            here = (
+                wave[pl.ds(z * GROUP, GROUP), at] * weight
+                - upper_mod[pl.ds(z * GROUP, GROUP), at] * later
+            )
+            solved[pl.ds(z * GROUP, 2 * GROUP), at] = jnp.concatenate(
+                [here, later], 0
+            ).astype(jnp.bfloat16)
+            if z > 0:
+                later = (
+                    wave[pl.ds((z - 1) * GROUP, GROUP), at] * weight
+                    - upper_mod[pl.ds((z - 1) * GROUP, GROUP), at] * here
+                )
+
+    @pl.loop(0, n_ha)
+    def _(step):
+        h = other_half_first(ha, step, n_ha)
+        back = lax.dot_general(
+            solved[...], x_table[pl.ds(pl.multiple_of(h * rows, rows), rows), :],
+            (((1,), (1,)), ((), ())), preferred_element_type=jnp.float32,
+        )
+        send2[h] = back.astype(jnp.bfloat16).reshape(n_gz, block_rows, rows)
+
+        @pl.loop(0, n_gz)
+        def _(turn):
+            g = (gz + 1 + turn) % n_gz
+
+            @pl.when(h * n_gz + g != me)
+            def _():
+                second_copy(h, g, me).start()
+
+    own_back = pltpu.make_async_copy(send2.at[ha, gz], recv2.at[me], own_sem.at[0])
+    own_back.start()
+    own_back.wait()
+
+    @pl.loop(1, count)
+    def _(step):
+        peer = (me + step) % count
+        second_copy(peer // n_gz, peer % n_gz, peer).wait_recv()
+
+    for z in range(depth):
+        part = recv2[:, pl.ds((z // 2) * 2 * GROUP, 2 * GROUP), :].astype(jnp.float32)
+        part = part[:, (z % 2) * GROUP:(z % 2 + 1) * GROUP, :]
+        out_ref[z] = part.reshape(count * GROUP, rows).astype(jnp.bfloat16)
+
+    @pl.loop(1, count)
+    def _(step):
+        peer = (me + step) % count
+        first_copy(peer // n_gz, peer % n_gz, ha, gz).wait_send()
+        second_copy(peer // n_gz, peer % n_gz, me).wait_send()
+
+    @pl.loop(1, n_gz)
+    def _(step):
+        coef_copy((gz + step) % n_gz, gz).wait_send()
+
+
+def body_channels(n_ha, n_gz, velocity, lower_coef, upper_coef):
+    depth, rows, _ = velocity.shape
+    count = n_ha * n_gz
+    bulk = depth * n_gz * GROUP
+    block_rows = depth * GROUP
+    cosine, sine = host_tables(NY, KYW)
+    y_table = jnp.asarray(np.concatenate([cosine.T, -sine.T], 0), jnp.bfloat16)
+    weight = np.where(np.arange(KYW) == 0, 1.0, 2.0)[:, None]
+    back_table = jnp.asarray(
+        np.concatenate([cosine.T * weight, -sine.T * weight], 0), jnp.bfloat16
+    )
+    x_table = real_x_table()
+    hbm = pl.BlockSpec(memory_space=pl.ANY)
+    smem = pl.BlockSpec(memory_space=pltpu.SMEM)
+    dma = pltpu.SemaphoreType.DMA
+    planes = pl.pallas_call(
+        functools.partial(middle_kernel, n_ha, n_gz, depth),
+        out_shape=jax.ShapeDtypeStruct((depth, count * GROUP, rows), jnp.bfloat16),
+        in_specs=[hbm, hbm, hbm, smem, smem],
+        out_specs=pl.BlockSpec(memory_space=pltpu.VMEM),
+        scratch_shapes=[
+            pltpu.VMEM(velocity.shape, jnp.bfloat16),
+            pltpu.VMEM(y_table.shape, jnp.bfloat16),
+            pltpu.VMEM(x_table.shape, jnp.bfloat16),
+            pltpu.VMEM((n_ha, n_gz, block_rows, rows), jnp.bfloat16),
+            pltpu.VMEM((n_ha, n_gz, block_rows, rows), jnp.bfloat16),
+            pltpu.VMEM((bulk, NX), jnp.float32),
+            pltpu.VMEM((bulk, NX), jnp.float32),
+            pltpu.VMEM((bulk, NX), jnp.float32),
+            pltpu.VMEM((bulk, NX), jnp.bfloat16),
+            pltpu.VMEM((n_ha, n_gz, block_rows, rows), jnp.bfloat16),
+            pltpu.VMEM((count, block_rows, rows), jnp.bfloat16),
+            pltpu.VMEM((2 * depth, LANES), jnp.float32),
+            pltpu.VMEM((n_gz, 2 * depth, LANES), jnp.float32),
+            dma((depth + 1,)), dma, dma((2,)),
+            dma((count,)), dma((count,)), dma((count,)), dma((count,)),
+            dma((n_gz,)), dma((n_gz,)),
+        ],
+        compiler_params=pltpu.CompilerParams(
+            collective_id=0, has_side_effects=True, vmem_limit_bytes=48 * 1024 * 1024
+        ),
+    )(velocity, y_table, x_table, lower_coef, upper_coef)
+    result = jnp.einsum("zkx,ky->zxy", planes, back_table, preferred_element_type=jnp.float32)
+    return result.astype(jnp.bfloat16)
+
+
 def solution(mesh):
+    n_ha, n_gz = mesh.shape["ha"], mesh.shape["gz"]
+    by_channel = (
+        2 * KYW == n_ha * n_gz * GROUP
+        and n_ha % 2 == 0
+        and NX % (n_ha * LANES) == 0
+    )
+    body = functools.partial(body_channels, n_ha, n_gz) if by_channel else body_general
     in_specs = (P("gz", "ha", None), P("gz"), P("gz"))
     out_specs = P("gz", "ha", None)
     return jax.shard_map(body, mesh=mesh, in_specs=in_specs, out_specs=out_specs, check_vma=False)

time: 471 us -> 45.9 us (0.10); the launches traced: 463 us -> 45.7 us
  matrix products: 276 us -> 3.3 us
  local copies, waits for them, and re-layouts: 91.2 us -> 4.72 us
  Pallas kernels: 0 us -> 37.6 us
  waiting for transfers between devices: 31.8 us -> 0 us
  other arithmetic: 27.7 us -> 0 us
  blocking collectives: 20.8 us -> 0 us
  starting transfers between devices: 13.9 us -> 0 us
    dot_general x8 -> x1, matrix products: 276 us -> 3.3 us  [body_channels(): jnp.einsum('zkx,ky->zxy', planes, back_table, preferred_element_type=jnp....]
    pallas_call x0 -> x1, Pallas kernels: none -> 37.6 us  [body_channels(): pl.pallas_call(functools.partial(middle_kernel, n_ha, n_gz, depth), out_s...]
    unnamed x15 -> x10, local copies, waits for them, and re-layouts: 39.2 us -> 4.72 us
    all_to_all x3 -> x0, waiting for transfers between devices: 31.8 us -> none  [the longest x1 15.2 us: body(): lax.all_to_all(planes, 'ha', split_axis=3, concat_axis=2, tiled=True)]
    dynamic_update_slice x48 -> x0, other arithmetic: 23.4 us -> none  [thomas(): lax.scan(forward, initial, (lower_band, main_band, upper_band, source))]
    all_to_all x7 -> x0, local copies, waits for them, and re-layouts: 20.9 us -> none  [the longest x2 10.6 us: body(): lax.all_to_all(source, 'gz', split_axis=3, concat_axis=0, tiled=True)]
    another operation x6 -> x0, local copies, waits for them, and re-layouts: 17 us -> none  [the longest x1 8.46 us: body(): jnp.stack([with_cos[:, 0] + with_sin[:, 1], with_cos[:, 1] - with_sin[:,...]
    all_to_all x3 -> x0, starting transfers between devices: 13.9 us -> none  [the longest x1 6.36 us: body(): lax.all_to_all(spectrum, 'ha', split_axis=2, concat_axis=3, tiled=True)]
  transfers between devices with their start and end apart: 3 -> 0, of which waited for: 3 -> 0; matrix products, arithmetic and copies ran while one was open for 0% -> 0% of each run, Pallas kernels for 0% -> 0%
where the time goes in v1:
time: 45.9 us; the launch traced here: 45.7 us
  Pallas kernels  37.6 us (82%)
  local copies, waits for them, and re-layouts  4.72 us (10%)
  matrix products  3.3 us (7%)
    pallas_call x1, Pallas kernels, body_channels(): pl.pallas_call(functools.partial(middle_kernel, n_ha, n_gz, depth), out_s...  37.6 us
    unnamed x10, local copies, waits for them, and re-layouts  4.72 us
    dot_general x1, matrix products, body_channels(): jnp.einsum('zkx,ky->zxy', planes, back_table, preferred_element_type=jnp....  3.3 us

profile of v1, /device:TPU:0, one launch (start us, length us, event | category | flops | bytes accessed | tf_op | source)
XLA Modules:
  0.0 45.7 jit_solution(7466196234119545975)
XLA Ops:
  0.0 0.0 copy-start
  0.0 2.2 %copy-done = bf16[4,256,2048]{2,1,0:T(8,128)(2,1)S(1)} copy-done((bf16[4,256,2048]{2,1,0:T(8,128)(2,1)S(1)}, bf16[4,256,2048]{2,1,0:T(8,128)(2,1)}, u32[]{:S(2)}) %copy-start) | copy-done | bytes 4194328
  2.2 0.0 copy-start.1
  2.2 1.2 %copy-done.1 = bf16[256,2048]{1,0:T(8,128)(2,1)S(1)} copy-done((bf16[256,2048]{1,0:T(8,128)(2,1)S(1)}, bf16[256,2048]{1,0:T(8,128)(2,1)}, u32[]{:S(2)}) %copy-start.1) | copy-done | bytes 1048600
  3.4 0.0 copy-start.2
  3.4 0.7 %copy-done.2 = f32[4]{0:T(128)S(1)} copy-done((f32[4]{0:T(128)S(1)}, f32[4]{0:T(128)}, u32[]{:S(2)}) %copy-start.2) | copy-done | bytes 40
  4.1 0.0 copy-start.3
  4.1 0.7 %copy-done.3 = f32[4]{0:T(128)S(1)} copy-done((f32[4]{0:T(128)S(1)}, f32[4]{0:T(128)}, u32[]{:S(2)}) %copy-start.3) | copy-done | bytes 40
  4.7 0.0 copy-start.4
  4.7 37.6 %shard_map.64 = bf16[4,256,256]{2,1,0:T(8,128)(2,1)S(1)} custom-call(bf16[4,256,2048]{2,1,0:T(8,128)(2,1)S(1)} %copy-done, bf16[256,2048]{1,0:T(8,128)(2,1)S(1)} %copy-done.1, bf16[2048,2048]{1,0:T(8,128)(2,1)} %constant.8.clone.x_table_ref, f32[4]{0:T(128)S(1)} %copy-done.2, f32[4]{0:T(128)S(1)} %copy-done.3), custom_call_target="tpu_custom_call" | custom-call | tf_op jit(solution)/shard_map/pallas_call | solution.py:411
  42.4 0.0 copy-done.4
  42.4 3.3 %convolution_convert_fusion = bf16[4,256,2048]{2,1,0:T(8,128)(2,1)} fusion(bf16[4,256,256]{2,1,0:T(8,128)(2,1)S(1)} %shard_map.64, bf16[256,2048,1]{1,0,2:T(8,128)(2,1)S(1)} %copy-done.4), kind=kOutput, calls=%fused_computation | convolution fusion | flops 1075838976 | bytes 5767168 | tf_op jit(solution)/shard_map/zkx,ky->zxy/dot_general | solution.py:438
Async XLA Ops:
  0.0 2.2 %copy-start = (bf16[4,256,2048]{2,1,0:T(8,128)(2,1)S(1)}, bf16[4,256,2048]{2,1,0:T(8,128)(2,1)}, u32[]{:S(2)}) copy-start(bf16[4,256,2048]{2,1,0:T(8,128)(2,1)} %velocity_ref.1) | copy-start | bytes 12582916
  2.2 1.2 %copy-start.1 = (bf16[256,2048]{1,0:T(8,128)(2,1)S(1)}, bf16[256,2048]{1,0:T(8,128)(2,1)}, u32[]{:S(2)}) copy-start(bf16[256,2048]{1,0:T(8,128)(2,1)} %constant.6.clone.y_table_ref) | copy-start | bytes 3145732
  3.4 0.7 %copy-start.2 = (f32[4]{0:T(128)S(1)}, f32[4]{0:T(128)}, u32[]{:S(2)}) copy-start(f32[4]{0:T(128)} %lower_ref.1) | copy-start | bytes 52
  4.1 0.7 %copy-start.3 = (f32[4]{0:T(128)S(1)}, f32[4]{0:T(128)}, u32[]{:S(2)}) copy-start(f32[4]{0:T(128)} %upper_ref.1) | copy-start | bytes 52
  4.7 37.6 %copy-start.4 = (bf16[256,2048,1]{1,0,2:T(8,128)(2,1)S(1)}, bf16[256,2048,1]{1,0,2:T(8,128)(2,1)}, u32[]{:S(2)}) copy-start(bf16[256,2048,1]{1,0,2:T(8,128)(2,1)} %constant.9) | copy-start | bytes 3145732

commit v2 on v1

--- a/solution.py
+++ b/solution.py
@@ -173,8 +173,6 @@
     z_total = depth * n_gz
     block_rows = depth * GROUP
     bulk = z_total * GROUP
-    half_ha = n_ha // 2
-    half_channels = half_ha * n_gz * GROUP
 
     y_load = pltpu.make_async_copy(y_table_ref, y_table, load_sem.at[depth])
     y_load.start()
@@ -231,37 +229,33 @@
         )
 
     y_load.wait()
-    for part in range(2):
-        side = (ha // half_ha + 1 + part) % 2
-        first = pl.multiple_of(side * half_channels, half_channels)
+    for pair in range(0, depth, 2):
         planes = []
-        for z in range(depth):
-            if part == 0:
-                loads[z].wait()
+        for z in range(pair, pair + 2):
+            loads[z].wait()
             planes.append(
                 lax.dot_general(
-                    y_table[pl.ds(first, half_channels), :], velocity[z],
+                    y_table[...], velocity[z],
                     (((1,), (1,)), ((), ())), preferred_element_type=jnp.float32,
-                ).reshape(half_ha, n_gz, 1, GROUP, rows)
+                ).reshape(n_ha, n_gz, 1, GROUP, rows)
             )
-        spectrum = jnp.concatenate(planes, 2).reshape(half_ha, n_gz, block_rows, rows)
-        send1[pl.ds(side * half_ha, half_ha)] = spectrum.astype(jnp.bfloat16)
-
-        if part == 0:
-            pl.semaphore_wait(barrier, count - 1)
-
-            @pl.loop(1, n_gz)
-            def _(step):
-                coef_copy((gz + step) % n_gz, gz).start()
-
-        @pl.loop(0, half_ha * n_gz)
-        def _(step):
-            h = side * half_ha + (ha + 1 + step // n_gz) % half_ha
-            g = (gz + 1 + step) % n_gz
-
-            @pl.when(h * n_gz + g != me)
-            def _():
-                first_copy(h, g, ha, gz).start()
+        spectrum = jnp.concatenate(planes, 2).reshape(n_ha, n_gz, 2 * GROUP, rows)
+        send1[:, :, pl.ds(pair * GROUP, 2 * GROUP), :] = spectrum.astype(jnp.bfloat16)
+
+    pl.semaphore_wait(barrier, count - 1)
+
+    @pl.loop(1, n_gz)
+    def _(step):
+        coef_copy((gz + step) % n_gz, gz).start()
+
+    @pl.loop(0, count)
+    def _(step):
+        h = other_half_first(ha, step // n_gz, n_ha)
+        g = (gz + 1 + step) % n_gz
+
+        @pl.when(h * n_gz + g != me)
+        def _():
+            first_copy(h, g, ha, gz).start()
 
     own = pltpu.make_async_copy(send1.at[ha, gz], recv1.at[ha, gz], own_sem.at[0])
     own.start()
@@ -432,7 +426,7 @@
             dma((n_gz,)), dma((n_gz,)),
         ],
         compiler_params=pltpu.CompilerParams(
-            collective_id=0, has_side_effects=True, vmem_limit_bytes=48 * 1024 * 1024
+            collective_id=0, has_side_effects=True, vmem_limit_bytes=60 * 1024 * 1024
         ),
     )(velocity, y_table, x_table, lower_coef, upper_coef)
     result = jnp.einsum("zkx,ky->zxy", planes, back_table, preferred_element_type=jnp.float32)

time: 45.9 us -> 43.6 us (0.950)
  local copies, waits for them, and re-layouts: 4.72 us -> 0.01 us
  Pallas kernels: 37.6 us -> 39.1 us
  matrix products: 3.3 us -> 4.34 us
    unnamed x10 -> x2, local copies, waits for them, and re-layouts: 4.72 us -> 0.01 us
    pallas_call x1, Pallas kernels: 37.6 us -> 39.1 us  [body_channels(): pl.pallas_call(functools.partial(middle_kernel, n_ha, n_gz, depth), out_s...]
    dot_general x1, matrix products: 3.3 us -> 4.34 us  [body_channels(): jnp.einsum('zkx,ky->zxy', planes, back_table, preferred_element_type=jnp....]
where the time goes in v2:
time: 43.6 us; the launch traced here: 43.5 us
  Pallas kernels  39.1 us (90%)
  matrix products  4.34 us (10%)
    pallas_call x1, Pallas kernels, body_channels(): pl.pallas_call(functools.partial(middle_kernel, n_ha, n_gz, depth), out_s...  39.1 us
    dot_general x1, matrix products, body_channels(): jnp.einsum('zkx,ky->zxy', planes, back_table, preferred_element_type=jnp....  4.34 us

profile of v2, /device:TPU:0, one launch (start us, length us, event | category | flops | bytes accessed | tf_op | source)
XLA Modules:
  0.0 43.5 jit_solution(12492743562790996250)
XLA Ops:
  0.0 0.0 copy-start
  0.0 39.1 %shard_map.64 = bf16[4,256,256]{2,1,0:T(8,128)(2,1)} custom-call(bf16[4,256,2048]{2,1,0:T(8,128)(2,1)} %velocity_ref.1, bf16[256,2048]{1,0:T(8,128)(2,1)} %constant.6.clone.y_table_ref, bf16[2048,2048]{1,0:T(8,128)(2,1)} %constant.8.clone.x_table_ref, f32[4]{0:T(128)} %lower_ref.1, f32[4]{0:T(128)} %upper_ref.1), custom_call_target="tpu_custom_call" | custom-call | tf_op jit(solution)/shard_map/pallas_call | solution.py:405
  39.1 0.0 copy-done
  39.1 4.3 %convolution_convert_fusion = bf16[4,256,2048]{2,1,0:T(8,128)(2,1)} fusion(bf16[4,256,256]{2,1,0:T(8,128)(2,1)} %shard_map.64, bf16[256,2048,1]{1,0,2:T(8,128)(2,1)S(1)} %copy-done), kind=kOutput, calls=%fused_computation | convolution fusion | flops 1075838976 | bytes 5767168 | tf_op jit(solution)/shard_map/zkx,ky->zxy/dot_general | solution.py:432
Async XLA Ops:
  0.0 39.1 %copy-start = (bf16[256,2048,1]{1,0,2:T(8,128)(2,1)S(1)}, bf16[256,2048,1]{1,0,2:T(8,128)(2,1)}, u32[]{:S(2)}) copy-start(bf16[256,2048,1]{1,0,2:T(8,128)(2,1)} %constant.9) | copy-start | bytes 3145732

commit v3 on v2

--- a/solution.py
+++ b/solution.py
@@ -248,14 +248,10 @@
     def _(step):
         coef_copy((gz + step) % n_gz, gz).start()
 
-    @pl.loop(0, count)
-    def _(step):
-        h = other_half_first(ha, step // n_gz, n_ha)
-        g = (gz + 1 + step) % n_gz
-
-        @pl.when(h * n_gz + g != me)
-        def _():
-            first_copy(h, g, ha, gz).start()
+    @pl.loop(1, count)
+    def _(step):
+        peer = (me + step) % count
+        first_copy(peer // n_gz, peer % n_gz, ha, gz).start()
 
     own = pltpu.make_async_copy(send1.at[ha, gz], recv1.at[ha, gz], own_sem.at[0])
     own.start()
@@ -366,15 +362,22 @@
     own_back.start()
     own_back.wait()
 
-    @pl.loop(1, count)
-    def _(step):
-        peer = (me + step) % count
-        second_copy(peer // n_gz, peer % n_gz, peer).wait_recv()
-
-    for z in range(depth):
-        part = recv2[:, pl.ds((z // 2) * 2 * GROUP, 2 * GROUP), :].astype(jnp.float32)
-        part = part[:, (z % 2) * GROUP:(z % 2 + 1) * GROUP, :]
-        out_ref[z] = part.reshape(count * GROUP, rows).astype(jnp.bfloat16)
+    @pl.loop(0, count // 2)
+    def _(step):
+        pair = (me // 2 + 1 + step) % (count // 2)
+        for member in range(2):
+            source = pair * 2 + member
+
+            @pl.when(source != me)
+            def _():
+                second_copy(source // n_gz, source % n_gz, source).wait_recv()
+
+        even = recv2[pair * 2].astype(jnp.float32)
+        odd = recv2[pair * 2 + 1].astype(jnp.float32)
+        at = pl.ds(pl.multiple_of(pair * 2 * GROUP, 2 * GROUP), 2 * GROUP)
+        for z in range(depth):
+            own_z = slice(z * GROUP, (z + 1) * GROUP)
+            out_ref[z, at, :] = jnp.concatenate([even[own_z], odd[own_z]], 0).astype(jnp.bfloat16)
 
     @pl.loop(1, count)
     def _(step):

time: 43.6 us -> 43.5 us (level)
  no operation moved by 1% of the time
where the time goes in v3:
time: 43.5 us; the launch traced here: 43.3 us
  Pallas kernels  38.9 us (89%)
  matrix products  4.34 us (10%)
    pallas_call x1, Pallas kernels, body_channels(): pl.pallas_call(functools.partial(middle_kernel, n_ha, n_gz, depth), out_s...  38.9 us
    dot_general x1, matrix products, body_channels(): jnp.einsum('zkx,ky->zxy', planes, back_table, preferred_element_type=jnp....  4.34 us

profile of v3, /device:TPU:0, one launch (start us, length us, event | category | flops | bytes accessed | tf_op | source)
XLA Modules:
  0.0 43.3 jit_solution(6593493261640703434)
XLA Ops:
  0.0 0.0 copy-start
  0.0 38.9 %shard_map.64 = bf16[4,256,256]{2,1,0:T(8,128)(2,1)} custom-call(bf16[4,256,2048]{2,1,0:T(8,128)(2,1)} %velocity_ref.1, bf16[256,2048]{1,0:T(8,128)(2,1)} %constant.6.clone.y_table_ref, bf16[2048,2048]{1,0:T(8,128)(2,1)} %constant.8.clone.x_table_ref, f32[4]{0:T(128)} %lower_ref.1, f32[4]{0:T(128)} %upper_ref.1), custom_call_target="tpu_custom_call" | custom-call | tf_op jit(solution)/shard_map/pallas_call | solution.py:408
  39.0 0.0 copy-done
  39.0 4.3 %convolution_convert_fusion = bf16[4,256,2048]{2,1,0:T(8,128)(2,1)} fusion(bf16[4,256,256]{2,1,0:T(8,128)(2,1)} %shard_map.64, bf16[256,2048,1]{1,0,2:T(8,128)(2,1)S(1)} %copy-done), kind=kOutput, calls=%fused_computation | convolution fusion | flops 1075838976 | bytes 5767168 | tf_op jit(solution)/shard_map/zkx,ky->zxy/dot_general | solution.py:435
Async XLA Ops:
  0.0 39.0 %copy-start = (bf16[256,2048,1]{1,0,2:T(8,128)(2,1)S(1)}, bf16[256,2048,1]{1,0,2:T(8,128)(2,1)}, u32[]{:S(2)}) copy-start(bf16[256,2048,1]{1,0,2:T(8,128)(2,1)} %constant.9) | copy-start | bytes 3145732
